TPU v7x, 256 devices: a whole 4x4x8 slice. The times are simulated.
256 devices in a mesh: seq: 16 (over y, x), chan: 16 (over z, core).
Axes of the slice: x: 4, y: 4, z: 8, core: 2. Of those that a mesh axis runs over, the one named last changes fastest.
Arguments:
- tokens: bfloat16 [57344, 2048], P('seq', 'chan'), may hold values from -6 to 6
- w_query: bfloat16 [2048, 256], replicated, may hold values from -0.125 to 0.125
- w_key: bfloat16 [2048, 256], replicated, may hold values from -0.125 to 0.125
- w_value: bfloat16 [2048, 2048], P(None, 'chan'), may hold values from -0.125 to 0.125
- w_out: bfloat16 [2048, 2048], replicated, may hold values from -0.125 to 0.125
- gain: float32 [2048], replicated, may hold values from 0.1 to 1.9
Outputs:
- mixed: bfloat16 [57344, 2048], P('seq', 'chan')
All inputs are finite; a program needn't handle non-finite values.
Results may differ from a plain program's by a relative error of at most 0.019.
Values may be sent and summed in bfloat16 or wider, within the bound.
A program may use at most 128 MiB of HBM per device.

v0:
```python
import jax
import jax.numpy as jnp
from jax import lax
from jax.sharding import PartitionSpec as P

HEADS = 16
FEAT = 16
HEAD_DIM = 128
BLOCK = 896


def feature_parts(rows):
    linear = rows * FEAT ** (-0.25)
    square = (rows[..., :, None] * rows[..., None, :]).reshape(rows.shape[:-1] + (FEAT * FEAT,)) * (
        2.0 * FEAT
    ) ** (-0.5)
    return (linear, square)


def per_device(tokens, w_query, w_key, w_value, w_out, gain):
    highest = lax.Precision.HIGHEST
    groups = lax.axis_size("chan")
    per_group = HEADS // groups
    my_group = lax.axis_index("chan")
    my_slab = lax.axis_index("seq")
    tok_rows = tokens.shape[0]
    query_cols = per_group * FEAT
    value_cols = per_group * HEAD_DIM
    query_mine = lax.dynamic_slice_in_dim(w_query, my_group * query_cols, query_cols, 1)
    key_mine = lax.dynamic_slice_in_dim(w_key, my_group * query_cols, query_cols, 1)
    initial = (
        jnp.zeros((tok_rows, query_cols), jnp.float32),
        jnp.zeros((tok_rows, query_cols), jnp.float32),
        jnp.zeros((tok_rows, value_cols), jnp.float32),
    )
    piece = lax.all_gather(tokens, "chan", axis=1, tiled=True)
    query_sum, key_sum, value_sum = tuple(
        (
            jnp.dot(piece, weight, preferred_element_type=jnp.float32)
            for weight in (query_mine, key_mine, w_value)
        )
    )
    query_rows = query_sum.astype(jnp.bfloat16)
    key_rows = key_sum.astype(jnp.bfloat16)
    value_rows = value_sum.astype(jnp.bfloat16)
    blocks = tok_rows // BLOCK
    query_blocks = query_rows.reshape(blocks, BLOCK, per_group, FEAT)
    key_blocks = key_rows.reshape(blocks, BLOCK, per_group, FEAT)
    value_blocks = value_rows.reshape(blocks, BLOCK, per_group, HEAD_DIM)
    value_f32 = value_blocks.astype(jnp.float32)
    key_linear, key_square = feature_parts(key_blocks.astype(jnp.float32))
    own_zero = jnp.sum(value_f32, axis=1)
    own_one = jnp.einsum("bthf,bthe->bhfe", key_linear, value_f32, precision=highest)
    own_two = jnp.einsum("bthf,bthe->bhfe", key_square, value_f32, precision=highest)
    own = (own_zero, own_one, own_two)
    slab_total = tuple((jnp.sum(member, axis=0) for member in own))
    initial = tuple((jnp.zeros_like(member) for member in slab_total))
    pieces = (
        lax.all_gather(slab_total[0][None].astype(jnp.bfloat16), "seq", axis=0, tiled=True).astype(
            jnp.float32
        ),
        lax.all_gather(slab_total[1][None].astype(jnp.bfloat16), "seq", axis=0, tiled=True).astype(
            jnp.float32
        ),
        lax.all_gather(slab_total[2][None].astype(jnp.bfloat16), "seq", axis=0, tiled=True).astype(
            jnp.float32
        ),
    )
    count = pieces[0].shape[0]
    order = jnp.arange(count, dtype=jnp.int32)
    earlier_mask = order < my_slab
    prefix = tuple(
        (
            total
            + jnp.sum(
                jnp.where(earlier_mask.reshape((count,) + (1,) * (piece.ndim - 1)), piece, 0.0),
                axis=0,
            )
            for total, piece in zip(initial, pieces)
        )
    )
    earlier = tuple(
        (
            jnp.concatenate([jnp.zeros_like(member[:1]), jnp.cumsum(member, axis=0)[:-1]], axis=0)
            + base[None]
            for member, base in zip(own, prefix)
        )
    )
    query_linear, query_square = feature_parts(query_blocks.astype(jnp.float32))
    inter = earlier[0][:, None] + jnp.einsum(
        "bthf,bhfe->bthe", query_linear, earlier[1], precision=highest
    )
    inter = inter + jnp.einsum("bthf,bhfe->bthe", query_square, earlier[2], precision=highest)
    scores = jnp.einsum(
        "bthf,bshf->bhts", query_blocks, key_blocks, preferred_element_type=jnp.float32
    ) * FEAT ** (-0.5)
    kernel = 1.0 + scores + 0.5 * scores * scores
    causal = jnp.arange(BLOCK)[:, None] >= jnp.arange(BLOCK)[None, :]
    weights = jnp.where(causal, kernel, 0.0).astype(jnp.bfloat16)
    intra = jnp.einsum("bhts,bshe->bthe", weights, value_blocks, preferred_element_type=jnp.float32)
    numerator = (intra + inter).reshape(tok_rows, per_group, HEAD_DIM)
    gain_mine = lax.dynamic_slice_in_dim(gain, my_group * value_cols, value_cols, 0).reshape(
        per_group, HEAD_DIM
    )
    mean_square = jnp.mean(numerator * numerator, axis=-1, keepdims=True)
    hidden = (
        (numerator * lax.rsqrt(mean_square + 1e-05) * gain_mine)
        .astype(jnp.bfloat16)
        .reshape(tok_rows, value_cols)
    )
    out_mine = lax.dynamic_slice_in_dim(w_out, my_group * value_cols, value_cols, 0)
    partial_value = jnp.dot(hidden, out_mine, preferred_element_type=jnp.float32)
    partial_value = lax.optimization_barrier(partial_value.astype(jnp.bfloat16)).astype(jnp.float32)
    mixed = lax.psum_scatter(
        partial_value.astype(jnp.bfloat16), "chan", scatter_dimension=1, tiled=True
    )
    return mixed


def solution(mesh):
    return jax.shard_map(
        per_device,
        mesh=mesh,
        in_specs=(P("seq", "chan"), P(), P(), P(None, "chan"), P(), P()),
        out_specs=P("seq", "chan"),
        check_vma=False,
    )
```

profile of v0, /device:TPU:2, one launch (start us, length us, event | category | flops | bytes accessed | tf_op | source)
XLA Modules:
  0.0 357.5 jit_solution(1797674125439511556)
XLA Ops:
  6.5 0.7 all-gather.7.cloned.1.call-update
  7.3 0.8 dynamic_slice.14
  8.3 96.7 %all-gather.7.cloned.1.call-done = bf16[3584,2048]{1,0:T(8,128)(2,1)} async-done(((bf16[3584,128]{1,0:T(8,128)(2,1)}), bf16[3584,2048]{1,0:T(8,128)(2,1)}) %all-gather.7.cloned.1.call-update) | async-done | bytes 14680080 | tf_op jit(solution)/shard_map/all_gather | solution.py:36
  105.0 9.2 %fusion.51 = (bf16[128]{0:T(256)(128)(2,1)S(1)}, bf16[3584,128]{1,0:T(8,128)(2,1)S(1)}) fusion(bf16[3584,2048]{1,0:T(8,128)(2,1)} %all-gather.7.cloned.1.call-done, bf16[2048,128]{1,0:T(8,128)(2,1)} %param.9), kind=kOutput, calls=%fused_computation.68 | convolution fusion | flops 1879965568 | bytes 16122112 | tf_op jit(solution)/shard_map/dot_general | solution.py:39
  114.4 9.4 %convolution_convert_fusion.2 = bf16[16,3584]{1,0:T(8,128)(2,1)S(1)} fusion(bf16[3584,2048]{1,0:T(8,128)(2,1)} %all-gather.7.cloned.1.call-done, bf16[2048,256]{1,0:T(8,128)(2,1)S(1)} %copy-done, s32[]{:T(128)S(6)} %select_n.25), kind=kOutput, calls=%fused_computation.3 | convolution fusion | flops 234938368 | bytes 15319044 | tf_op jit(solution)/shard_map/dot_general | solution.py:39
  123.8 0.5 fusion.50
  124.4 20.3 %all-gather.3 = bf16[16,1,128]{2,1,0:T(2,128)(2,1)S(1)} all-gather(bf16[1,1,128]{2,1,0:T(2,128)(2,1)S(1)} %bitcast.100), channel_id=2, replica_groups=mesh['seq'=16,'chan'=16] {'seq'}, dimensions={0}, use_global_device_ids=true | all-gather | bytes 4352 | tf_op jit(solution)/shard_map/all_gather | solution.py:59
  144.8 21.4 %all-gather.1 = bf16[256,128]{1,0:T(8,128)(2,1)S(1)} all-gather(bf16[16,128]{1,0:T(8,128)(2,1)S(1)} %get-tuple-element.7), channel_id=3, replica_groups=mesh['seq'=16,'chan'=16] {'seq'}, dimensions={0}, use_global_device_ids=true | all-gather | bytes 69632 | tf_op jit(solution)/shard_map/all_gather | solution.py:62
  166.2 0.4 multiply_multiply_fusion.1
  166.6 2.5 fusion.49
  169.1 0.4 fusion.8
  169.8 9.6 %convolution_convert_fusion.3 = bf16[16,3584]{1,0:T(8,128)(2,1)S(1)} fusion(bf16[3584,2048]{1,0:T(8,128)(2,1)} %all-gather.7.cloned.1.call-done, bf16[2048,256]{1,0:T(8,128)(2,1)} %param.7, s32[]{:T(128)S(6)} %select_n.25), kind=kOutput, calls=%fused_computation.4 | convolution fusion | flops 234938368 | bytes 15319044 | tf_op jit(solution)/shard_map/dot_general | solution.py:39
  179.4 2.9 fusion.16
  182.3 2.2 multiply_multiply_fusion
  184.5 29.4 %all-gather.9.cloned.1.call-done = bf16[4096,128]{1,0:T(8,128)(2,1)} async-done(((bf16[256,128]{1,0:T(8,128)(2,1)}), bf16[4096,128]{1,0:T(8,128)(2,1)}) %all-gather.9.cloned.1.call-update) | async-done | bytes 1048592 | tf_op jit(solution)/shard_map/all_gather | solution.py:65
  213.9 1.5 fusion
  215.4 5.6 %fusion.6 = f32[4,128,896]{2,1,0:T(8,128)} fusion(f32[4,896,256]{1,2,0:T(8,128)} %bitcast.84, f32[3,1,256,128]{3,2,0,1:T(8,128)S(1)} %slice-done, f32[256,128]{1,0:T(8,128)S(1)} %fusion), kind=kOutput, calls=%fused_computation.20 | convolution fusion | flops 1409417216 | bytes 6029312 | tf_op jit(solution)/shard_map/bthf,bhfe->bthe/dot_general | solution.py:93
  221.0 8.5 %multiply_reduce_fusion = (f32[4,896]{1,0:T(4,128)S(1)}, f32[4,896,1,128]{1,3,0,2:T(8,128)}) fusion(f32[4,128,896]{2,1,0:T(8,128)} %fusion.6, f32[4,128,896]{2,1,0:T(8,128)} %fusion.16, f32[4,128]{1,0:T(4,128)S(1)} %add_bitcast_fusion, bf16[4,896,128]{2,1,0:T(8,128)(2,1)S(1)} %bitcast.88, pred[896,896]{1,0:T(8,128)(4,1)S(1)} %iota_compare_fusion, ...), kind=kOutput, calls=%fused_computation.18 | convolution fusion | flops 949613056 | bytes 7471104 | tf_op jit(solution)/shard_map/bhts,bshe->bthe/dot_general | solution.py:100
  229.5 1.8 copy.41
  231.3 0.5 fusion.3
  231.9 8.3 %convolution_convert_fusion = bf16[3584,2048]{1,0:T(8,128)(2,1)} fusion(bf16[3584,128]{1,0:T(8,128)(2,1)S(1)} %fusion.3, bf16[2048,2048]{1,0:T(8,128)(2,1)} %param.10, s32[]{:T(128)S(6)} %select_n.30), kind=kOutput, calls=%fused_computation | convolution fusion | flops 1886388224 | bytes 16121860 | tf_op jit(solution)/shard_map/dot_general | solution.py:112
  240.2 18.8 %copy.45 = bf16[3584,2048]{0,1:T(8,128)(2,1)} copy(bf16[3584,2048]{1,0:T(8,128)(2,1)} %convolution_convert_fusion) | data formatting | bytes 29360128
  259.0 89.8 %reduce-scatter.4.cloned.1.call-done = bf16[128,3584]{1,0:T(8,128)(2,1)} async-done(((bf16[2048,3584]{1,0:T(8,128)(2,1)}), bf16[128,3584]{1,0:T(8,128)(2,1)}) %reduce-scatter.4.cloned.1.call-update) | async-done | bytes 917520
  348.8 2.2 copy.46
  (29 shorter events, 0.9 us)
Async XLA Ops:
  6.5 107.9 %copy-start = (bf16[2048,256]{1,0:T(8,128)(2,1)S(1)}, bf16[2048,256]{1,0:T(8,128)(2,1)}, u32[]{:S(2)}) copy-start(bf16[2048,256]{1,0:T(8,128)(2,1)} %param.8) | copy-start | bytes 3145732
  6.5 98.5 %all-gather.7.cloned.1.call-start = ((), (), s32[]{:S(2)}) async-start(), calls=%async_computation.1 | async-start | bytes 15597568 | tf_op jit(solution)/shard_map/all_gather | solution.py:36
  7.3 206.7 %all-gather.9.cloned.1.call-start = ((), (), s32[]{:S(2)}) async-start(), calls=%async_computation.2 | async-start | bytes 1114112 | tf_op jit(solution)/shard_map/all_gather | solution.py:65
  144.8 24.3 %copy-start.3 = (f32[4,1,16,128]{3,2,0,1:T(8,128)}, f32[4,1,16,128]{3,2,0,1:T(8,128)S(1)}, u32[]{:S(2)}) copy-start(f32[4,1,16,128]{3,2,0,1:T(8,128)S(1)} %fusion.32) | copy-start | bytes 98308
  169.1 179.7 %reduce-scatter.4.cloned.1.call-start = ((), (), s32[]{:S(2)}) async-start(), calls=%async_computation.3 | async-start | bytes 15597568
  169.5 9.9 %copy-start.2 = (f32[4,1,256,128]{3,2,0,1:T(8,128)}, f32[4,1,256,128]{3,2,0,1:T(8,128)S(1)}, u32[]{:S(2)}) copy-start(f32[4,1,256,128]{3,2,0,1:T(8,128)S(1)} %fusion.8) | copy-start | bytes 1572868
  169.8 9.6 %slice-start.1 = ((f32[4,1,16,128]{3,2,0,1:T(8,128)}), f32[3,1,16,128]{3,2,0,1:T(8,128)S(1)}, s32[]{:S(2)}) async-start(f32[4,1,16,128]{3,2,0,1:T(8,128)} %copy-done.3), calls=%async_computation.5 | async-start | bytes 49152 | tf_op jit(solution)/shard_map/slice | solution.py:84
  179.4 36.0 %slice-start = ((f32[4,1,256,128]{3,2,0,1:T(8,128)}), f32[3,1,256,128]{3,2,0,1:T(8,128)S(1)}, s32[]{:S(2)}) async-start(f32[4,1,256,128]{3,2,0,1:T(8,128)} %copy-done.2), calls=%async_computation.4 | async-start | bytes 786432 | tf_op jit(solution)/shard_map/slice | solution.py:84
  259.0 92.0 %copy-start.1 = (bf16[2048,256]{1,0:T(8,128)(2,1)S(1)}, bf16[2048,256]{1,0:T(8,128)(2,1)}, u32[]{:S(2)}) copy-start(bf16[2048,256]{1,0:T(8,128)(2,1)} %param.8) | copy-start | bytes 3145732
Sparse Core Ops, SparseCore 0:
  9.1 95.8 all-gather.6
  169.2 44.6 all-gather.8
  259.1 89.6 reduce-scatter.3
where the time goes:
time: 358 us
  waiting for transfers between devices  217 us (61%)
  matrix products  56.4 us (16%)
  blocking collectives  41.7 us (12%)
  local copies, waits for them, and re-layouts  23.6 us (7%)
  between operations  13.3 us (4%)
  other arithmetic  5.75 us (2%)
    all_gather x1, waiting for transfers between devices, per_device(): piece = lax.all_gather(tokens, 'chan', axis=1, tiled=True)  96.7 us
    unnamed x4, waiting for transfers between devices  90.5 us
    all_gather x1, waiting for transfers between devices, per_device(): lax.all_gather(slab_total[2][None].astype(jnp.bfloat16), 'seq', axis=0, t...  29.4 us
    dot_general x3, matrix products, per_device(): jnp.dot(piece, weight, preferred_element_type=jnp.float32)  28.2 us
    all_gather x1, blocking collectives, per_device(): lax.all_gather(slab_total[1][None].astype(jnp.bfloat16), 'seq', axis=0, t...  21.4 us
    unnamed x10, local copies, waits for them, and re-layouts  21 us
    all_gather x1, blocking collectives, per_device(): lax.all_gather(slab_total[0][None].astype(jnp.bfloat16), 'seq', axis=0, t...  20.3 us
    dot_general x1, matrix products, per_device(): jnp.einsum('bhts,bshe->bthe', weights, value_blocks, preferred_element_ty...  8.45 us
  transfers between devices with their start and end apart: 3, of which 3 were waited for; matrix products, arithmetic and copies ran while one was open for 5% of the time, Pallas kernels for 0%

commit v1 on v0

--- a/solution.py
+++ b/solution.py
@@ -33,7 +33,12 @@
         jnp.zeros((tok_rows, query_cols), jnp.float32),
         jnp.zeros((tok_rows, value_cols), jnp.float32),
     )
-    piece = lax.all_gather(tokens, "chan", axis=1, tiled=True)
+    ring = [tokens]
+    for hop in range(15):
+        ring.append(lax.ppermute(ring[-1], "chan", [(dev, (dev + 1) % 16) for dev in range(16)]))
+    piece = jnp.roll(
+        jnp.concatenate(ring[::-1], axis=1), (lax.axis_index("chan") + 1) * ring[0].shape[1], axis=1
+    )
     query_sum, key_sum, value_sum = tuple(
         (
             jnp.dot(piece, weight, preferred_element_type=jnp.float32)

time: 358 us -> 507 us (1.42)
  waiting for transfers between devices: 217 us -> 300 us
  local copies, waits for them, and re-layouts: 23.6 us -> 88.9 us
    ppermute x0 -> x15, waiting for transfers between devices: none -> 211 us  [per_device(): lax.ppermute(ring[-1], 'chan', [(dev, (dev + 1) % 16) for dev in range(16)])]
    all_gather x1 -> x0, waiting for transfers between devices: 96.7 us -> none  [per_device(): piece = lax.all_gather(tokens, 'chan', axis=1, tiled=True)]
    unnamed x10 -> x87, local copies, waits for them, and re-layouts: 21 us -> 85.1 us
    all_gather x1, waiting for transfers between devices: 29.4 us -> 0.01 us  [per_device(): lax.all_gather(slab_total[2][None].astype(jnp.bfloat16), 'seq', axis=0, t...]
    unnamed x4 -> x3, waiting for transfers between devices: 90.5 us -> 89 us
  transfers between devices with their start and end apart: 3 -> 17, of which waited for: 3 -> 16; matrix products, arithmetic and copies ran while one was open for 5% -> 3% of each run, Pallas kernels for 0% -> 0%
where the time goes in v1:
time: 507 us; the launch traced here: 506 us
  waiting for transfers between devices  300 us (59%)
  local copies, waits for them, and re-layouts  88.9 us (18%)
  matrix products  54.3 us (11%)
  blocking collectives  42.2 us (8%)
  between operations  13.7 us (3%)
  other arithmetic  6.54 us (1%)
    ppermute x15, waiting for transfers between devices, per_device(): lax.ppermute(ring[-1], 'chan', [(dev, (dev + 1) % 16) for dev in range(16)])  211 us
    unnamed x3, waiting for transfers between devices  89 us
    unnamed x87, local copies, waits for them, and re-layouts  85.1 us
    dot_general x3, matrix products, per_device(): jnp.dot(piece, weight, preferred_element_type=jnp.float32)  26.2 us
    all_gather x1, blocking collectives, per_device(): lax.all_gather(slab_total[1][None].astype(jnp.bfloat16), 'seq', axis=0, t...  21.6 us
    all_gather x1, blocking collectives, per_device(): lax.all_gather(slab_total[0][None].astype(jnp.bfloat16), 'seq', axis=0, t...  20.6 us
  transfers between devices with their start and end apart: 17, of which 16 were waited for; matrix products, arithmetic and copies ran while one was open for 3% of the time, Pallas kernels for 0%

profile of v1, /device:TPU:2, one launch (start us, length us, event | category | flops | bytes accessed | tf_op | source)
XLA Modules:
  0.0 505.9 jit_solution(1647778096592941649)
XLA Ops:
  6.6 16.6 %collective-permute-done = bf16[3584,128]{1,0:T(8,128)(2,1)S(1)} collective-permute-done((bf16[3584,128]{1,0:T(8,128)(2,1)}, bf16[3584,128]{1,0:T(8,128)(2,1)S(1)}, u32[]{:S(2)}, u32[]{:S(2)}) %collective-permute-start) | collective-permute-done | bytes 917536 | tf_op jit(solution)/shard_map/ppermute | solution.py:38
  23.2 14.0 %collective-permute-done.1 = bf16[3584,128]{1,0:T(8,128)(2,1)S(1)} collective-permute-done((bf16[3584,128]{1,0:T(8,128)(2,1)S(1)}, bf16[3584,128]{1,0:T(8,128)(2,1)S(1)}, u32[]{:S(2)}, u32[]{:S(2)}) %collective-permute-start.1) | collective-permute-done | bytes 917536 | tf_op jit(solution)/shard_map/ppermute | solution.py:38
  38.2 14.0 %collective-permute-done.2 = bf16[3584,128]{1,0:T(8,128)(2,1)S(1)} collective-permute-done((bf16[3584,128]{1,0:T(8,128)(2,1)S(1)}, bf16[3584,128]{1,0:T(8,128)(2,1)S(1)}, u32[]{:S(2)}, u32[]{:S(2)}) %collective-permute-start.2) | collective-permute-done | bytes 917536 | tf_op jit(solution)/shard_map/ppermute | solution.py:38
  53.1 14.0 %collective-permute-done.3 = bf16[3584,128]{1,0:T(8,128)(2,1)S(1)} collective-permute-done((bf16[3584,128]{1,0:T(8,128)(2,1)S(1)}, bf16[3584,128]{1,0:T(8,128)(2,1)S(1)}, u32[]{:S(2)}, u32[]{:S(2)}) %collective-permute-start.3) | collective-permute-done | bytes 917536 | tf_op jit(solution)/shard_map/ppermute | solution.py:38
  68.1 14.0 %collective-permute-done.4 = bf16[3584,128]{1,0:T(8,128)(2,1)S(1)} collective-permute-done((bf16[3584,128]{1,0:T(8,128)(2,1)S(1)}, bf16[3584,128]{1,0:T(8,128)(2,1)S(1)}, u32[]{:S(2)}, u32[]{:S(2)}) %collective-permute-start.4) | collective-permute-done | bytes 917536 | tf_op jit(solution)/shard_map/ppermute | solution.py:38
  83.1 14.0 %collective-permute-done.5 = bf16[3584,128]{1,0:T(8,128)(2,1)S(1)} collective-permute-done((bf16[3584,128]{1,0:T(8,128)(2,1)S(1)}, bf16[3584,128]{1,0:T(8,128)(2,1)S(1)}, u32[]{:S(2)}, u32[]{:S(2)}) %collective-permute-start.5) | collective-permute-done | bytes 917536 | tf_op jit(solution)/shard_map/ppermute | solution.py:38
  98.1 14.0 %collective-permute-done.6 = bf16[3584,128]{1,0:T(8,128)(2,1)S(1)} collective-permute-done((bf16[3584,128]{1,0:T(8,128)(2,1)S(1)}, bf16[3584,128]{1,0:T(8,128)(2,1)S(1)}, u32[]{:S(2)}, u32[]{:S(2)}) %collective-permute-start.6) | collective-permute-done | bytes 917536 | tf_op jit(solution)/shard_map/ppermute | solution.py:38
  113.0 14.0 %collective-permute-done.7 = bf16[3584,128]{1,0:T(8,128)(2,1)S(1)} collective-permute-done((bf16[3584,128]{1,0:T(8,128)(2,1)S(1)}, bf16[3584,128]{1,0:T(8,128)(2,1)S(1)}, u32[]{:S(2)}, u32[]{:S(2)}) %collective-permute-start.7) | collective-permute-done | bytes 917536 | tf_op jit(solution)/shard_map/ppermute | solution.py:38
  128.0 14.0 %collective-permute-done.8 = bf16[3584,128]{1,0:T(8,128)(2,1)S(1)} collective-permute-done((bf16[3584,128]{1,0:T(8,128)(2,1)S(1)}, bf16[3584,128]{1,0:T(8,128)(2,1)S(1)}, u32[]{:S(2)}, u32[]{:S(2)}) %collective-permute-start.8) | collective-permute-done | bytes 917536 | tf_op jit(solution)/shard_map/ppermute | solution.py:38
  143.0 14.0 %collective-permute-done.9 = bf16[3584,128]{1,0:T(8,128)(2,1)S(1)} collective-permute-done((bf16[3584,128]{1,0:T(8,128)(2,1)S(1)}, bf16[3584,128]{1,0:T(8,128)(2,1)S(1)}, u32[]{:S(2)}, u32[]{:S(2)}) %collective-permute-start.9) | collective-permute-done | bytes 917536 | tf_op jit(solution)/shard_map/ppermute | solution.py:38
  158.0 14.0 %collective-permute-done.10 = bf16[3584,128]{1,0:T(8,128)(2,1)S(1)} collective-permute-done((bf16[3584,128]{1,0:T(8,128)(2,1)S(1)}, bf16[3584,128]{1,0:T(8,128)(2,1)S(1)}, u32[]{:S(2)}, u32[]{:S(2)}) %collective-permute-start.10) | collective-permute-done | bytes 917536 | tf_op jit(solution)/shard_map/ppermute | solution.py:38
  172.9 14.0 %collective-permute-done.11 = bf16[3584,128]{1,0:T(8,128)(2,1)S(1)} collective-permute-done((bf16[3584,128]{1,0:T(8,128)(2,1)S(1)}, bf16[3584,128]{1,0:T(8,128)(2,1)S(1)}, u32[]{:S(2)}, u32[]{:S(2)}) %collective-permute-start.11) | collective-permute-done | bytes 917536 | tf_op jit(solution)/shard_map/ppermute | solution.py:38
  187.9 14.0 %collective-permute-done.12 = bf16[3584,128]{1,0:T(8,128)(2,1)S(1)} collective-permute-done((bf16[3584,128]{1,0:T(8,128)(2,1)S(1)}, bf16[3584,128]{1,0:T(8,128)(2,1)S(1)}, u32[]{:S(2)}, u32[]{:S(2)}) %collective-permute-start.12) | collective-permute-done | bytes 917536 | tf_op jit(solution)/shard_map/ppermute | solution.py:38
  202.9 14.1 %collective-permute-done.13 = bf16[3584,128]{1,0:T(8,128)(2,1)} collective-permute-done((bf16[3584,128]{1,0:T(8,128)(2,1)S(1)}, bf16[3584,128]{1,0:T(8,128)(2,1)}, u32[]{:S(2)}, u32[]{:S(2)}) %collective-permute-start.13) | collective-permute-done | bytes 917536 | tf_op jit(solution)/shard_map/ppermute | solution.py:38
  219.2 12.1 %collective-permute-done.14 = bf16[3584,128]{1,0:T(8,128)(2,1)} collective-permute-done((bf16[3584,128]{1,0:T(8,128)(2,1)}, bf16[3584,128]{1,0:T(8,128)(2,1)}, u32[]{:S(2)}, u32[]{:S(2)}) %collective-permute-start.14) | collective-permute-done | bytes 917536 | tf_op jit(solution)/shard_map/ppermute | solution.py:38
  285.2 7.8 %fusion.67 = (bf16[128]{0:T(256)(128)(2,1)S(1)}, bf16[3584,128]{1,0:T(8,128)(2,1)S(1)}) fusion(bf16[2048,128]{1,0:T(8,128)(2,1)S(1)} %copy-done.26, bf16[3584,4096]{1,0:T(8,128)(2,1)} %constant_dynamic-update-slice_fusion, s32[]{:T(128)S(6)} %select_n.39), kind=kOutput, calls=%fused_computation.107 | convolution fusion | flops 1879965568 | bytes 16122116 | tf_op jit(solution)/shard_map/dot_general | solution.py:44
  293.0 9.1 %fusion.12 = bf16[3584,16]{0,1:T(8,128)(2,1)S(1)} fusion(bf16[3584,4096]{1,0:T(8,128)(2,1)} %constant_dynamic-update-slice_fusion, s32[]{:T(128)S(6)} %select_n.39, bf16[2048,256]{1,0:T(8,128)(2,1)S(1)} %copy-done, s32[]{:T(128)S(6)} %select_n.40), kind=kOutput, calls=%fused_computation.10 | convolution fusion | flops 234938368 | bytes 15319048 | tf_op jit(solution)/shard_map/dot_general | solution.py:44
  306.2 20.6 %all-gather.3 = bf16[16,1,128]{2,1,0:T(2,128)(2,1)S(1)} all-gather(bf16[1,1,128]{2,1,0:T(2,128)(2,1)S(1)} %bitcast.95), channel_id=2, replica_groups=mesh['seq'=16,'chan'=16] {'seq'}, dimensions={0}, use_global_device_ids=true | all-gather | bytes 4352 | tf_op jit(solution)/shard_map/all_gather | solution.py:64
  326.8 21.6 %all-gather.1 = bf16[256,128]{1,0:T(8,128)(2,1)S(1)} all-gather(bf16[16,128]{1,0:T(8,128)(2,1)S(1)} %get-tuple-element.7), channel_id=3, replica_groups=mesh['seq'=16,'chan'=16] {'seq'}, dimensions={0}, use_global_device_ids=true | all-gather | bytes 69632 | tf_op jit(solution)/shard_map/all_gather | solution.py:67
  348.6 9.3 %fusion.9 = bf16[3584,16]{0,1:T(8,128)(2,1)S(1)} fusion(bf16[3584,4096]{1,0:T(8,128)(2,1)} %constant_dynamic-update-slice_fusion, s32[]{:T(128)S(6)} %select_n.39, bf16[2048,256]{1,0:T(8,128)(2,1)} %param.7, s32[]{:T(128)S(6)} %select_n.40), kind=kOutput, calls=%fused_computation.9 | convolution fusion | flops 234938368 | bytes 15319048 | tf_op jit(solution)/shard_map/dot_general | solution.py:44
  370.0 8.4 %multiply_reduce_fusion = (f32[4,896]{1,0:T(4,128)S(1)}, f32[4,896,1,128]{1,3,0,2:T(8,128)}) fusion(f32[4,128,896]{2,1,0:T(8,128)} %fusion.21, f32[4,128,896]{2,1,0:T(8,128)} %fusion.31, f32[4,128]{1,0:T(4,128)S(1)} %add_bitcast_fusion, bf16[4,896,128]{2,1,0:T(8,128)(2,1)S(1)} %bitcast.83, pred[896,896]{1,0:T(8,128)(4,1)} %iota_compare_fusion, ...), kind=kOutput, calls=%fused_computation.24 | convolution fusion | flops 949613056 | bytes 7471104 | tf_op jit(solution)/shard_map/bhts,bshe->bthe/dot_general | solution.py:105
  380.8 8.3 %convolution_convert_fusion = bf16[3584,2048]{1,0:T(8,128)(2,1)} fusion(bf16[3584,128]{1,0:T(8,128)(2,1)S(1)} %fusion.18, bf16[2048,2048]{1,0:T(8,128)(2,1)} %param.10, s32[]{:T(128)S(6)} %select_n.45), kind=kOutput, calls=%fused_computation | convolution fusion | flops 1886388224 | bytes 16121860 | tf_op jit(solution)/shard_map/dot_general | solution.py:117
  389.1 18.8 %copy.45 = bf16[3584,2048]{0,1:T(8,128)(2,1)} copy(bf16[3584,2048]{1,0:T(8,128)(2,1)} %convolution_convert_fusion) | data formatting | bytes 29360128
  407.9 89.0 %reduce-scatter.4.cloned.1.call-done = bf16[128,3584]{1,0:T(8,128)(2,1)} async-done(((bf16[2048,3584]{1,0:T(8,128)(2,1)}), bf16[128,3584]{1,0:T(8,128)(2,1)}) %reduce-scatter.4.cloned.1.call-update) | async-done | bytes 917520
  (132 shorter events, 88.3 us)
Async XLA Ops:
  6.5 286.4 %copy-start = (bf16[2048,256]{1,0:T(8,128)(2,1)S(1)}, bf16[2048,256]{1,0:T(8,128)(2,1)}, u32[]{:S(2)}) copy-start(bf16[2048,256]{1,0:T(8,128)(2,1)} %param.8) | copy-start | bytes 3145732
  6.5 277.6 %copy-start.1 = (bf16[3584,128]{1,0:T(8,128)(2,1)S(1)}, bf16[3584,128]{1,0:T(8,128)(2,1)}, u32[]{:S(2)}) copy-start(bf16[3584,128]{1,0:T(8,128)(2,1)} %param.6) | copy-start | bytes 2752516
  6.5 356.4 %all-gather.6.cloned.1.call-start = ((), (), s32[]{:S(2)}) async-start(), calls=%async_computation.1 | async-start | bytes 1114112 | tf_op jit(solution)/shard_map/all_gather | solution.py:70
  6.5 16.6 %collective-permute-start = (bf16[3584,128]{1,0:T(8,128)(2,1)}, bf16[3584,128]{1,0:T(8,128)(2,1)S(1)}, u32[]{:S(2)}, u32[]{:S(2)}) collective-permute-start(bf16[3584,128]{1,0:T(8,128)(2,1)} %param.6), channel_id=1, source_target_pairs={{0,1},{1,2},{2,3},{3,4},{4,5},{5,6},{6,7},{7,8},{8,9},{9,10},{10,1... | collective-permute-start | bytes 2752520 | tf_op jit(solution)/shard_map/ppermute | solution.py:38
  23.2 14.0 %collective-permute-start.1 = (bf16[3584,128]{1,0:T(8,128)(2,1)S(1)}, bf16[3584,128]{1,0:T(8,128)(2,1)S(1)}, u32[]{:S(2)}, u32[]{:S(2)}) collective-permute-start(bf16[3584,128]{1,0:T(8,128)(2,1)S(1)} %collective-permute-done), channel_id=1, source_target_pairs={{0,1},{1,2},{2,3},{3,4},{4,5},{5,6},{6,7},{7,8},{8,9},{9,10},{10,1... | collective-permute-start | bytes 2752520 | tf_op jit(solution)/shard_map/ppermute | solution.py:38
  38.2 14.0 %collective-permute-start.2 = (bf16[3584,128]{1,0:T(8,128)(2,1)S(1)}, bf16[3584,128]{1,0:T(8,128)(2,1)S(1)}, u32[]{:S(2)}, u32[]{:S(2)}) collective-permute-start(bf16[3584,128]{1,0:T(8,128)(2,1)S(1)} %collective-permute-done.1), channel_id=1, source_target_pairs={{0,1},{1,2},{2,3},{3,4},{4,5},{5,6},{6,7},{7,8},{8,9},{9,10},{10,1... | collective-permute-start | bytes 2752520 | tf_op jit(solution)/shard_map/ppermute | solution.py:38
  53.1 14.0 %collective-permute-start.3 = (bf16[3584,128]{1,0:T(8,128)(2,1)S(1)}, bf16[3584,128]{1,0:T(8,128)(2,1)S(1)}, u32[]{:S(2)}, u32[]{:S(2)}) collective-permute-start(bf16[3584,128]{1,0:T(8,128)(2,1)S(1)} %collective-permute-done.2), channel_id=1, source_target_pairs={{0,1},{1,2},{2,3},{3,4},{4,5},{5,6},{6,7},{7,8},{8,9},{9,10},{10,1... | collective-permute-start | bytes 2752520 | tf_op jit(solution)/shard_map/ppermute | solution.py:38
  68.1 14.0 %collective-permute-start.4 = (bf16[3584,128]{1,0:T(8,128)(2,1)S(1)}, bf16[3584,128]{1,0:T(8,128)(2,1)S(1)}, u32[]{:S(2)}, u32[]{:S(2)}) collective-permute-start(bf16[3584,128]{1,0:T(8,128)(2,1)S(1)} %collective-permute-done.3), channel_id=1, source_target_pairs={{0,1},{1,2},{2,3},{3,4},{4,5},{5,6},{6,7},{7,8},{8,9},{9,10},{10,1... | collective-permute-start | bytes 2752520 | tf_op jit(solution)/shard_map/ppermute | solution.py:38
  83.1 14.0 %collective-permute-start.5 = (bf16[3584,128]{1,0:T(8,128)(2,1)S(1)}, bf16[3584,128]{1,0:T(8,128)(2,1)S(1)}, u32[]{:S(2)}, u32[]{:S(2)}) collective-permute-start(bf16[3584,128]{1,0:T(8,128)(2,1)S(1)} %collective-permute-done.4), channel_id=1, source_target_pairs={{0,1},{1,2},{2,3},{3,4},{4,5},{5,6},{6,7},{7,8},{8,9},{9,10},{10,1... | collective-permute-start | bytes 2752520 | tf_op jit(solution)/shard_map/ppermute | solution.py:38
  98.1 14.0 %collective-permute-start.6 = (bf16[3584,128]{1,0:T(8,128)(2,1)S(1)}, bf16[3584,128]{1,0:T(8,128)(2,1)S(1)}, u32[]{:S(2)}, u32[]{:S(2)}) collective-permute-start(bf16[3584,128]{1,0:T(8,128)(2,1)S(1)} %collective-permute-done.5), channel_id=1, source_target_pairs={{0,1},{1,2},{2,3},{3,4},{4,5},{5,6},{6,7},{7,8},{8,9},{9,10},{10,1... | collective-permute-start | bytes 2752520 | tf_op jit(solution)/shard_map/ppermute | solution.py:38
  113.0 14.0 %collective-permute-start.7 = (bf16[3584,128]{1,0:T(8,128)(2,1)S(1)}, bf16[3584,128]{1,0:T(8,128)(2,1)S(1)}, u32[]{:S(2)}, u32[]{:S(2)}) collective-permute-start(bf16[3584,128]{1,0:T(8,128)(2,1)S(1)} %collective-permute-done.6), channel_id=1, source_target_pairs={{0,1},{1,2},{2,3},{3,4},{4,5},{5,6},{6,7},{7,8},{8,9},{9,10},{10,1... | collective-permute-start | bytes 2752520 | tf_op jit(solution)/shard_map/ppermute | solution.py:38
  128.0 14.0 %collective-permute-start.8 = (bf16[3584,128]{1,0:T(8,128)(2,1)S(1)}, bf16[3584,128]{1,0:T(8,128)(2,1)S(1)}, u32[]{:S(2)}, u32[]{:S(2)}) collective-permute-start(bf16[3584,128]{1,0:T(8,128)(2,1)S(1)} %collective-permute-done.7), channel_id=1, source_target_pairs={{0,1},{1,2},{2,3},{3,4},{4,5},{5,6},{6,7},{7,8},{8,9},{9,10},{10,1... | collective-permute-start | bytes 2752520 | tf_op jit(solution)/shard_map/ppermute | solution.py:38
  142.9 14.0 %collective-permute-start.9 = (bf16[3584,128]{1,0:T(8,128)(2,1)S(1)}, bf16[3584,128]{1,0:T(8,128)(2,1)S(1)}, u32[]{:S(2)}, u32[]{:S(2)}) collective-permute-start(bf16[3584,128]{1,0:T(8,128)(2,1)S(1)} %collective-permute-done.8), channel_id=1, source_target_pairs={{0,1},{1,2},{2,3},{3,4},{4,5},{5,6},{6,7},{7,8},{8,9},{9,10},{10,1... | collective-permute-start | bytes 2752520 | tf_op jit(solution)/shard_map/ppermute | solution.py:38
  158.0 14.0 %collective-permute-start.10 = (bf16[3584,128]{1,0:T(8,128)(2,1)S(1)}, bf16[3584,128]{1,0:T(8,128)(2,1)S(1)}, u32[]{:S(2)}, u32[]{:S(2)}) collective-permute-start(bf16[3584,128]{1,0:T(8,128)(2,1)S(1)} %collective-permute-done.9), channel_id=1, source_target_pairs={{0,1},{1,2},{2,3},{3,4},{4,5},{5,6},{6,7},{7,8},{8,9},{9,10},{10,1... | collective-permute-start | bytes 2752520 | tf_op jit(solution)/shard_map/ppermute | solution.py:38
  172.9 14.0 %collective-permute-start.11 = (bf16[3584,128]{1,0:T(8,128)(2,1)S(1)}, bf16[3584,128]{1,0:T(8,128)(2,1)S(1)}, u32[]{:S(2)}, u32[]{:S(2)}) collective-permute-start(bf16[3584,128]{1,0:T(8,128)(2,1)S(1)} %collective-permute-done.10), channel_id=1, source_target_pairs={{0,1},{1,2},{2,3},{3,4},{4,5},{5,6},{6,7},{7,8},{8,9},{9,10},{10,1... | collective-permute-start | bytes 2752520 | tf_op jit(solution)/shard_map/ppermute | solution.py:38
  187.9 14.0 %collective-permute-start.12 = (bf16[3584,128]{1,0:T(8,128)(2,1)S(1)}, bf16[3584,128]{1,0:T(8,128)(2,1)S(1)}, u32[]{:S(2)}, u32[]{:S(2)}) collective-permute-start(bf16[3584,128]{1,0:T(8,128)(2,1)S(1)} %collective-permute-done.11), channel_id=1, source_target_pairs={{0,1},{1,2},{2,3},{3,4},{4,5},{5,6},{6,7},{7,8},{8,9},{9,10},{10,1... | collective-permute-start | bytes 2752520 | tf_op jit(solution)/shard_map/ppermute | solution.py:38
  202.9 14.1 %collective-permute-start.13 = (bf16[3584,128]{1,0:T(8,128)(2,1)S(1)}, bf16[3584,128]{1,0:T(8,128)(2,1)}, u32[]{:S(2)}, u32[]{:S(2)}) collective-permute-start(bf16[3584,128]{1,0:T(8,128)(2,1)S(1)} %collective-permute-done.12), channel_id=1, source_target_pairs={{0,1},{1,2},{2,3},{3,4},{4,5},{5,6},{6,7},{7,8},{8,9},{9,10},{10,1... | collective-permute-start | bytes 2752520 | tf_op jit(solution)/shard_map/ppermute | solution.py:38
  217.0 14.3 %collective-permute-start.14 = (bf16[3584,128]{1,0:T(8,128)(2,1)}, bf16[3584,128]{1,0:T(8,128)(2,1)}, u32[]{:S(2)}, u32[]{:S(2)}) collective-permute-start(bf16[3584,128]{1,0:T(8,128)(2,1)} %collective-permute-done.13), channel_id=1, source_target_pairs={{0,1},{1,2},{2,3},{3,4},{4,5},{5,6},{6,7},{7,8},{8,9},{9,10},{10,1... | collective-permute-start | bytes 2752520 | tf_op jit(solution)/shard_map/ppermute | solution.py:38
  217.1 61.8 %copy-start.9 = (bf16[3584,128]{1,0:T(8,128)(2,1)S(1)}, bf16[3584,128]{1,0:T(8,128)(2,1)}, u32[]{:S(2)}) copy-start(bf16[3584,128]{1,0:T(8,128)(2,1)} %copy-done.8) | copy-start | bytes 2752516
  217.1 62.8 %copy-start.7 = (bf16[3584,128]{1,0:T(8,128)(2,1)S(1)}, bf16[3584,128]{1,0:T(8,128)(2,1)}, u32[]{:S(2)}) copy-start(bf16[3584,128]{1,0:T(8,128)(2,1)} %copy-done.6) | copy-start | bytes 2752516
  217.1 63.9 %copy-start.5 = (bf16[3584,128]{1,0:T(8,128)(2,1)S(1)}, bf16[3584,128]{1,0:T(8,128)(2,1)}, u32[]{:S(2)}) copy-start(bf16[3584,128]{1,0:T(8,128)(2,1)} %copy-done.4) | copy-start | bytes 2752516
  217.1 65.0 %copy-start.3 = (bf16[3584,128]{1,0:T(8,128)(2,1)S(1)}, bf16[3584,128]{1,0:T(8,128)(2,1)}, u32[]{:S(2)}) copy-start(bf16[3584,128]{1,0:T(8,128)(2,1)} %copy-done.2) | copy-start | bytes 2752516
  219.2 66.0 %copy-start.26 = (bf16[2048,128]{1,0:T(8,128)(2,1)S(1)}, bf16[2048,128]{1,0:T(8,128)(2,1)}, u32[]{:S(2)}) copy-start(bf16[2048,128]{1,0:T(8,128)(2,1)} %param.9) | copy-start | bytes 1572868
  305.7 191.2 %reduce-scatter.4.cloned.1.call-start = ((), (), s32[]{:S(2)}) async-start(), calls=%async_computation.2 | async-start | bytes 15597568
  (20 other events, 467.8 us)
Sparse Core Ops, SparseCore 0:
  305.8 47.8 all-gather.5
  408.0 88.8 reduce-scatter.3
